TPU v7x, 32 devices: a whole 2x2x4 slice. The times are simulated.
32 devices in a mesh: sec: 4 (over y, x), tile: 8 (over z, core).
Axes of the slice: x: 2, y: 2, z: 4, core: 2. Of those that a mesh axis runs over, the one named last changes fastest.
Arguments:
- displacement: float32 [2, 16, 256, 256], P(None, 'sec', 'tile'), may hold values from -3 to 3
- coupling: float32 [4, 16, 256, 256], P(None, 'sec', 'tile'), may hold values from 0.1 to 1
- matches: float32 [4, 2, 16, 256, 256], P(None, None, 'sec', 'tile'), may hold values from -3 to 3
- step_sizes: float32 [2, 8], replicated, may hold values from 0.1 to 0.35
- restarts: int32 [2, 8], replicated, may hold values 0 or 1
- images: float32 [4, 64, 256, 256], P('sec', 'tile'), may hold values from 0 to 1
- block_anchor: int32 [4, 64], P('sec', 'tile'), may hold values from 0 to 32767
- block_dest: int32 [4, 64, 1], P('sec', 'tile'), may hold values from 0 to 7; in each aligned block of 8 rows (0 to 7, 8 to 15, ..., all dimensions but the last counted through in order) at most 2 rows name the same one
- block_slot: int32 [4, 64], P('sec', 'tile'), may hold values from 0 to 1
- block_offset: int32 [4, 64, 2], P('sec', 'tile'), may hold values from 0 to 128
- block_count: int32 [4, 8], P('sec', 'tile'), may hold values from 6 to 8, as said below
Outputs:
- aligned: float32 [2, 16, 256, 256], P(None, 'sec', 'tile')
- spans: float32 [64, 384, 384], P(('sec', 'tile'))
Inputs may be any that keep to these rules, and one draw needn't show every extreme that they name: `block_dest`: no tile index is named by more than 2 of the block slots of one device, and 2 is reached. `block_count`: some device uses all 8 slots.
All inputs are finite; a program needn't handle non-finite values.
Results may differ from a plain program's by a relative error of at most 0.0003.
Values sent between devices are 32-bit elements; how exact they have to be, the bound alone decides.
A program may use at most 128 MiB of HBM per device.

v0:
```python
import jax
import jax.numpy as jnp
from jax import lax
from jax.sharding import PartitionSpec as P

OUTER = 2
FIRE_STEPS = 8
BPP = 256
CH = 384
SPAN_DEV = 2
STIFFNESS = 1.0
MIXING = 0.1
EPSILON = 1e-06
SPEED_CAP = 0.1
PRECISE = lax.Precision.HIGHEST


def with_halo(array, sides, width):
    for axis, dim in sides:
        size, length = (lax.axis_size(axis), array.shape[dim])
        up = [(i, (i + 1) % size) for i in range(size - 1)]
        down = [(j, i) for i, j in up]
        last = lax.slice_in_dim(array, length - width, length, axis=dim)
        leading = lax.slice_in_dim(array, 0, width, axis=dim)
        before = lax.ppermute(last, axis, up)
        after = lax.ppermute(leading, axis, down)
        array = jnp.concatenate([before, array, after], axis=dim)
    return array


def forces(current, refer, coupling, matches, first_sec, sections_all):
    strain = current - refer
    rimmed = with_halo(strain, (("tile", 2),), 1)
    sides = jnp.pad(strain, ((0, 0), (0, 0), (0, 0), (1, 1)))
    summed = STIFFNESS * (
        rimmed[:, :, 2:] + rimmed[:, :, :-2] + sides[..., 2:] + sides[..., :-2] - 4.0 * strain
    )
    stacked = with_halo(current, (("sec", 1),), 2)
    sections_dev = current.shape[1]
    section = first_sec + jnp.arange(sections_dev)
    for which_k, reach in enumerate((-2, -1, 1, 2)):
        beside = stacked[:, 2 + reach : 2 + reach + sections_dev]
        usable = ((section + reach >= 0) & (section + reach < sections_all)).astype(jnp.float32)
        summed = summed + usable[None, :, None, None] * coupling[which_k][None] * (
            beside + matches[which_k] - current
        )
    return summed


def hat_rows(shift, size, source):
    row_pos = jnp.arange(size).astype(jnp.float32)[None, :, None]
    src_pos = jnp.arange(source).astype(jnp.float32)[None, None, :]
    return jnp.maximum(0.0, 1.0 - jnp.abs(row_pos - src_pos - shift[:, None, None]))


def warp_blocks(blocks_in, shift_y, shift_x):
    row_hats = hat_rows(shift_y, CH, BPP)
    col_hats = hat_rows(shift_x, CH, BPP)
    halfway = jnp.einsum("bij,bkj->bik", blocks_in, col_hats, precision=PRECISE)
    return jnp.einsum("bri,bik->brk", row_hats, halfway, precision=PRECISE)


def body(
    displacement,
    coupling,
    matches,
    step_sizes,
    restarts,
    images,
    block_anchor,
    block_dest,
    block_slot,
    block_offset,
    block_count,
):
    sections_dev = displacement.shape[1]
    first_sec = lax.axis_index("sec") * sections_dev
    sections_all = sections_dev * lax.axis_size("sec")
    node_total = 2.0 * sections_all * displacement.shape[3] * displacement.shape[3]
    current = displacement
    refer = displacement
    velocity = jnp.zeros_like(displacement)
    for outer_step in range(OUTER):
        for inner_step in range(FIRE_STEPS):
            delta = step_sizes[outer_step, inner_step]
            push = forces(current, refer, coupling, matches, first_sec, sections_all)
            velocity = velocity + delta * push
            speed_sq, push_sq = lax.psum(
                (jnp.sum(velocity * velocity), jnp.sum(push * push)), ("sec", "tile")
            )
            ratio = jnp.sqrt(speed_sq + EPSILON) / jnp.sqrt(push_sq + EPSILON)
            limit = jnp.minimum(1.0, SPEED_CAP / jnp.sqrt(speed_sq / node_total + EPSILON))
            retain = 1.0 - restarts[outer_step, inner_step].astype(jnp.float32)
            velocity = limit * retain * ((1.0 - MIXING) * velocity + MIXING * ratio * push)
            current = current + delta * velocity
        refer = current
        velocity = jnp.zeros_like(current)
    flat_disp = current.reshape(2, -1)
    moved = jnp.take(flat_disp, block_anchor[0], axis=1)
    blocks_here = block_anchor.shape[1]
    usable = (jnp.arange(blocks_here) < block_count[0, 0]).astype(jnp.float32)
    offsets = block_offset[0].astype(jnp.float32)
    shift_y = offsets[:, 0] + moved[0]
    shift_x = offsets[:, 1] + moved[1]
    owners = block_dest[0, :, 0]
    slot_hot = (block_slot[0][:, None] == jnp.arange(SPAN_DEV)[None, :]).astype(
        jnp.float32
    ) * usable[:, None]
    tiles = lax.axis_size("tile")
    capacity = max(2, 2 * blocks_here // tiles)
    owner_hot = (owners[:, None] == jnp.arange(tiles)[None, :]).astype(jnp.int32)
    rank_all = jnp.cumsum(owner_hot, axis=0) - owner_hot
    rank_own = jnp.sum(rank_all * owner_hot, axis=1)
    position = owners * capacity + rank_own
    placer = (position[None, :] == jnp.arange(tiles * capacity)[:, None]).astype(jnp.float32)
    send_blocks = jnp.einsum("sb,bij->sij", placer, images[0], precision=PRECISE).reshape(
        tiles, capacity, BPP, BPP
    )
    shifts_both = jnp.stack([shift_y, shift_x], axis=1)
    send_shift = jnp.dot(placer, shifts_both, precision=PRECISE).reshape(tiles, capacity, 2)
    send_select = jnp.dot(placer, slot_hot, precision=PRECISE).reshape(tiles, capacity, SPAN_DEV)
    blocks_in = lax.all_to_all(send_blocks, "tile", split_axis=0, concat_axis=0, tiled=True)
    shift_in = lax.all_to_all(send_shift, "tile", split_axis=0, concat_axis=0, tiled=True)
    select_in = lax.all_to_all(send_select, "tile", split_axis=0, concat_axis=0, tiled=True)
    sources = blocks_in.shape[0]
    items = blocks_in.shape[1]
    drawn = warp_blocks(
        blocks_in.reshape(sources * items, BPP, BPP),
        shift_in[..., 0].reshape(-1),
        shift_in[..., 1].reshape(-1),
    )
    drawn = drawn.reshape(sources, items, CH, CH)
    pieces = jnp.einsum("skc,skrq->kcrq", select_in, drawn, precision=PRECISE)
    spans = jnp.sum(pieces, axis=0)
    return (current, spans)


def solution(mesh):
    placed = (
        P(None, "sec", "tile", None),
        P(None, "sec", "tile", None),
        P(None, None, "sec", "tile", None),
        P(),
        P(),
        P("sec", "tile", None, None),
        P("sec", "tile"),
        P("sec", "tile", None),
        P("sec", "tile"),
        P("sec", "tile", None),
        P("sec", "tile"),
    )
    return jax.shard_map(
        body,
        mesh=mesh,
        in_specs=placed,
        out_specs=(P(None, "sec", "tile", None), P(("sec", "tile"), None, None)),
        check_vma=False,
    )
```

profile of v0, /device:TPU:0, one launch (start us, length us, event | category | flops | bytes accessed | tf_op | source)
XLA Modules:
  0.0 1109.9 jit_solution(523799049433969451)
XLA Ops:
  1.8 4.9 collective-permute-start.2
  23.0 43.6 %all-reduce.31 = (f32[]{:T(128)}, f32[]{:T(128)}) all-reduce(f32[]{:T(128)} %get-tuple-element.41, f32[]{:T(128)} %get-tuple-element.40), channel_id=1, replica_groups=mesh['sec'=4,'tile'=8] {'sec','tile'}, use_global_device_ids=true, to_apply=%region_1.2 | all-reduce | flops 2 | bytes 16 | tf_op jit(solution)/shard_map/psum | solution.py:88
  69.4 4.2 collective-permute-start.6
  83.4 42.6 %all-reduce.30 = (f32[]{:T(128)}, f32[]{:T(128)}) all-reduce(f32[]{:T(128)} %get-tuple-element.39, f32[]{:T(128)} %get-tuple-element.38), channel_id=1, replica_groups=mesh['sec'=4,'tile'=8] {'sec','tile'}, use_global_device_ids=true, to_apply=%region_5.6 | all-reduce | flops 2 | bytes 16 | tf_op jit(solution)/shard_map/psum | solution.py:88
  142.7 41.5 %all-reduce.29 = (f32[]{:T(128)}, f32[]{:T(128)}) all-reduce(f32[]{:T(128)} %get-tuple-element.37, f32[]{:T(128)} %get-tuple-element.36), channel_id=1, replica_groups=mesh['sec'=4,'tile'=8] {'sec','tile'}, use_global_device_ids=true, to_apply=%region_9.10 | all-reduce | flops 2 | bytes 16 | tf_op jit(solution)/shard_map/psum | solution.py:88
  200.4 42.6 %all-reduce.28 = (f32[]{:T(128)}, f32[]{:T(128)}) all-reduce(f32[]{:T(128)} %get-tuple-element.35, f32[]{:T(128)} %get-tuple-element.34), channel_id=1, replica_groups=mesh['sec'=4,'tile'=8] {'sec','tile'}, use_global_device_ids=true, to_apply=%region_13.14 | all-reduce | flops 2 | bytes 16 | tf_op jit(solution)/shard_map/psum | solution.py:88
  245.7 4.2 collective-permute-start.18
  259.0 41.5 %all-reduce.27 = (f32[]{:T(128)}, f32[]{:T(128)}) all-reduce(f32[]{:T(128)} %get-tuple-element.33, f32[]{:T(128)} %get-tuple-element.32), channel_id=1, replica_groups=mesh['sec'=4,'tile'=8] {'sec','tile'}, use_global_device_ids=true, to_apply=%region_17.18 | all-reduce | flops 2 | bytes 16 | tf_op jit(solution)/shard_map/psum | solution.py:88
  316.8 42.6 %all-reduce.26 = (f32[]{:T(128)}, f32[]{:T(128)}) all-reduce(f32[]{:T(128)} %get-tuple-element.31, f32[]{:T(128)} %get-tuple-element.30), channel_id=1, replica_groups=mesh['sec'=4,'tile'=8] {'sec','tile'}, use_global_device_ids=true, to_apply=%region_21.22 | all-reduce | flops 2 | bytes 16 | tf_op jit(solution)/shard_map/psum | solution.py:88
  375.4 41.5 %all-reduce.25 = (f32[]{:T(128)}, f32[]{:T(128)}) all-reduce(f32[]{:T(128)} %get-tuple-element.29, f32[]{:T(128)} %get-tuple-element.28), channel_id=1, replica_groups=mesh['sec'=4,'tile'=8] {'sec','tile'}, use_global_device_ids=true, to_apply=%region_25.26 | all-reduce | flops 2 | bytes 16 | tf_op jit(solution)/shard_map/psum | solution.py:88
  433.0 42.6 %all-reduce.24 = (f32[]{:T(128)}, f32[]{:T(128)}) all-reduce(f32[]{:T(128)} %get-tuple-element.27, f32[]{:T(128)} %get-tuple-element.26), channel_id=1, replica_groups=mesh['sec'=4,'tile'=8] {'sec','tile'}, use_global_device_ids=true, to_apply=%region_29.30 | all-reduce | flops 2 | bytes 16 | tf_op jit(solution)/shard_map/psum | solution.py:88
  478.4 4.2 collective-permute-start.34
  491.6 41.4 %all-reduce.23 = (f32[]{:T(128)}, f32[]{:T(128)}) all-reduce(f32[]{:T(128)} %get-tuple-element.25, f32[]{:T(128)} %get-tuple-element.24), channel_id=1, replica_groups=mesh['sec'=4,'tile'=8] {'sec','tile'}, use_global_device_ids=true, to_apply=%region_33.34 | all-reduce | flops 2 | bytes 16 | tf_op jit(solution)/shard_map/psum | solution.py:88
  535.7 4.2 collective-permute-start.38
  549.6 42.6 %all-reduce.22 = (f32[]{:T(128)}, f32[]{:T(128)}) all-reduce(f32[]{:T(128)} %get-tuple-element.23, f32[]{:T(128)} %get-tuple-element.22), channel_id=1, replica_groups=mesh['sec'=4,'tile'=8] {'sec','tile'}, use_global_device_ids=true, to_apply=%region_37.38 | all-reduce | flops 2 | bytes 16 | tf_op jit(solution)/shard_map/psum | solution.py:88
  612.3 42.3 %all-reduce.21 = (f32[]{:T(128)}, f32[]{:T(128)}) all-reduce(f32[]{:T(128)} %get-tuple-element.21, f32[]{:T(128)} %get-tuple-element.20), channel_id=1, replica_groups=mesh['sec'=4,'tile'=8] {'sec','tile'}, use_global_device_ids=true, to_apply=%region_41.42 | all-reduce | flops 2 | bytes 16 | tf_op jit(solution)/shard_map/psum | solution.py:88
  657.4 4.2 collective-permute-start.46
  670.8 42.6 %all-reduce.20 = (f32[]{:T(128)}, f32[]{:T(128)}) all-reduce(f32[]{:T(128)} %get-tuple-element.19, f32[]{:T(128)} %get-tuple-element.18), channel_id=1, replica_groups=mesh['sec'=4,'tile'=8] {'sec','tile'}, use_global_device_ids=true, to_apply=%region_45.46 | all-reduce | flops 2 | bytes 16 | tf_op jit(solution)/shard_map/psum | solution.py:88
  729.3 41.5 %all-reduce.19 = (f32[]{:T(128)}, f32[]{:T(128)}) all-reduce(f32[]{:T(128)} %get-tuple-element.17, f32[]{:T(128)} %get-tuple-element.16), channel_id=1, replica_groups=mesh['sec'=4,'tile'=8] {'sec','tile'}, use_global_device_ids=true, to_apply=%region_49.50 | all-reduce | flops 2 | bytes 16 | tf_op jit(solution)/shard_map/psum | solution.py:88
  773.7 4.2 collective-permute-start.54
  787.0 42.6 %all-reduce.18 = (f32[]{:T(128)}, f32[]{:T(128)}) all-reduce(f32[]{:T(128)} %get-tuple-element.15, f32[]{:T(128)} %get-tuple-element.14), channel_id=1, replica_groups=mesh['sec'=4,'tile'=8] {'sec','tile'}, use_global_device_ids=true, to_apply=%region_53.54 | all-reduce | flops 2 | bytes 16 | tf_op jit(solution)/shard_map/psum | solution.py:88
  845.6 41.7 %all-reduce.17 = (f32[]{:T(128)}, f32[]{:T(128)}) all-reduce(f32[]{:T(128)} %get-tuple-element.13, f32[]{:T(128)} %get-tuple-element.12), channel_id=1, replica_groups=mesh['sec'=4,'tile'=8] {'sec','tile'}, use_global_device_ids=true, to_apply=%region_57.58 | all-reduce | flops 2 | bytes 16 | tf_op jit(solution)/shard_map/psum | solution.py:88
  890.0 4.2 collective-permute-start.62
  903.2 42.6 %all-reduce.16 = (f32[]{:T(128)}, f32[]{:T(128)}) all-reduce(f32[]{:T(128)} %get-tuple-element.11, f32[]{:T(128)} %get-tuple-element.10), channel_id=1, replica_groups=mesh['sec'=4,'tile'=8] {'sec','tile'}, use_global_device_ids=true, to_apply=%region_61.62 | all-reduce | flops 2 | bytes 16 | tf_op jit(solution)/shard_map/psum | solution.py:88
  948.4 8.5 copy.33
  957.0 6.3 gather_fusion
  967.9 4.3 fusion.20
  975.5 5.1 all-to-all-start.2
  981.0 93.7 %all-to-all-done.2 = f32[8,2,256,256]{3,2,1,0:T(8,128)} async-done(((f32[8,2,256,256]{3,2,1,0:T(8,128)}), f32[8,2,256,256]{3,2,1,0:T(8,128)}, u32[]{:S(2)}, u32[]{:S(2)}) %all-to-all-start.2) | async-done | bytes 4194336 | tf_op jit(solution)/shard_map/all_to_all | solution.py:122
  1074.7 10.7 fusion.2
  1085.4 12.1 %fusion.7 = f32[16,384,384]{2,1,0:T(8,128)S(1)} fusion(f32[16,256,384]{2,1,0:T(8,128)S(1)} %fusion.2, f32[16]{0:T(128)S(1)} %sub.587, f32[384,256]{1,0:T(8,128)S(1)} %broadcast_subtract_fusion), kind=kOutput, calls=%fused_computation.8 | convolution fusion | flops 7254048768 | bytes 16121920 | tf_op jit(solution)/shard_map/bri,bik->brk/dot_general | solution.py:60
  1097.5 11.1 fusion.23
  (236 shorter events, 203.0 us)
Async XLA Ops:
  1.8 12.1 %collective-permute-start.2 = (f32[2,2,32,256]{3,2,1,0:T(8,128)S(1)}, f32[2,2,32,256]{3,2,1,0:T(8,128)S(1)}, u32[]{:S(2)}, u32[]{:S(2)}) collective-permute-start(f32[2,2,32,256]{3,2,1,0:T(8,128)S(1)} %get-tuple-element.205), channel_id=1, source_target_pairs={{0,8},{8,16},{16,24},{1,9},{9,17},{17,25},{2,10},{10,18},{18,26},{... | collective-permute-start | bytes 393224 | tf_op jit(solution)/shard_map/ppermute | solution.py:25
  6.6 12.6 %collective-permute-start.3 = (f32[2,2,32,256]{3,2,1,0:T(8,128)S(1)}, f32[2,2,32,256]{3,2,1,0:T(8,128)S(1)}, u32[]{:S(2)}, u32[]{:S(2)}) collective-permute-start(f32[2,2,32,256]{3,2,1,0:T(8,128)S(1)} %get-tuple-element.206), channel_id=1, source_target_pairs={{8,0},{16,8},{24,16},{9,1},{17,9},{25,17},{10,2},{18,10},{26,18},{... | collective-permute-start | bytes 393224 | tf_op jit(solution)/shard_map/ppermute | solution.py:26
  69.4 10.7 collective-permute-start.6
  73.6 7.4 collective-permute-start.7
  129.3 10.7 collective-permute-start.10
  187.1 10.7 collective-permute-start.14
  191.3 7.5 collective-permute-start.15
  245.7 10.7 collective-permute-start.18
  303.4 10.7 collective-permute-start.22
  307.6 7.5 collective-permute-start.23
  362.2 10.7 collective-permute-start.26
  366.4 7.5 collective-permute-start.27
  419.6 10.8 collective-permute-start.30
  423.8 7.4 collective-permute-start.31
  478.4 11.2 %collective-permute-start.34 = (f32[2,2,32,256]{3,2,1,0:T(8,128)S(1)}, f32[2,2,32,256]{3,2,1,0:T(8,128)S(1)}, u32[]{:S(2)}, u32[]{:S(2)}) collective-permute-start(f32[2,2,32,256]{3,2,1,0:T(8,128)S(1)} %get-tuple-element.172), channel_id=1, source_target_pairs={{0,8},{8,16},{16,24},{1,9},{9,17},{17,25},{2,10},{10,18},{18,26},{... | collective-permute-start | bytes 393224 | tf_op jit(solution)/shard_map/ppermute | solution.py:25
  482.6 7.4 collective-permute-start.35
  535.7 10.7 collective-permute-start.38
  595.8 14.8 %collective-permute-start.42 = (f32[2,2,32,256]{3,2,1,0:T(8,128)S(1)}, f32[2,2,32,256]{3,2,1,0:T(8,128)S(1)}, u32[]{:S(2)}, u32[]{:S(2)}) collective-permute-start(f32[2,2,32,256]{3,2,1,0:T(8,128)S(1)} %get-tuple-element.164), channel_id=1, source_target_pairs={{0,8},{8,16},{16,24},{1,9},{9,17},{17,25},{2,10},{10,18},{18,26},{... | collective-permute-start | bytes 393224 | tf_op jit(solution)/shard_map/ppermute | solution.py:25
  600.0 10.6 collective-permute-start.43
  601.3 9.3 collective-permute-start.40
  602.6 8.0 collective-permute-start.41
  606.5 357.9 %all-to-all-start = ((f32[8,2,2]{2,1,0:T(2,128)}), f32[8,2,2]{2,1,0:T(2,128)S(1)}, u32[]{:S(2)}, u32[]{:S(2)}) async-start(f32[8,2,2]{2,1,0:T(2,128)} %bitcast.43), calls=%async_computation | async-start | bytes 16384 | tf_op jit(solution)/shard_map/all_to_all | solution.py:124
  657.4 10.7 collective-permute-start.46
  661.6 7.4 collective-permute-start.47
  716.0 10.7 collective-permute-start.50
  773.7 10.7 collective-permute-start.54
  777.9 7.4 collective-permute-start.55
  832.4 10.7 collective-permute-start.58
  836.6 7.4 collective-permute-start.59
  890.0 10.7 collective-permute-start.62
  964.4 11.1 %all-to-all-start.1 = ((f32[8,2,2]{1,2,0:T(2,128)}), f32[8,2,2]{1,2,0:T(2,128)S(1)}, u32[]{:S(2)}, u32[]{:S(2)}) async-start(f32[8,2,2]{1,2,0:T(2,128)} %copy.34), calls=%async_computation.1 | async-start | bytes 16384 | tf_op jit(solution)/shard_map/all_to_all | solution.py:123
  975.5 99.2 %all-to-all-start.2 = ((f32[8,2,256,256]{3,2,1,0:T(8,128)}), f32[8,2,256,256]{3,2,1,0:T(8,128)}, u32[]{:S(2)}, u32[]{:S(2)}) async-start(f32[8,2,256,256]{3,2,1,0:T(8,128)} %copy.36), calls=%async_computation.2 | async-start | bytes 8388608 | tf_op jit(solution)/shard_map/all_to_all | solution.py:122
  (42 other events, 934.3 us)
where the time goes:
time: 1120 us; the launch traced here: 1110 us
  blocking collectives  676 us (60%)
  starting transfers between devices  170 us (15%)
  waiting for transfers between devices  109 us (10%)
  other arithmetic  45.2 us (4%)
  between operations  44.9 us (4%)
  matrix products  39.1 us (3%)
  local copies, waits for them, and re-layouts  26 us (2%)
    psum x16, blocking collectives, body(): lax.psum((jnp.sum(velocity * velocity), jnp.sum(push * push)), ('sec', 't...  676 us
    ppermute x32, starting transfers between devices, with_halo(): before = lax.ppermute(last, axis, up)  116 us
    all_to_all x1, waiting for transfers between devices, body(): lax.all_to_all(send_blocks, 'tile', split_axis=0, concat_axis=0, tiled=True)  93.7 us
    ppermute x32, starting transfers between devices, with_halo(): after = lax.ppermute(leading, axis, down)  41.3 us
    reduce_sum x16, other arithmetic, body(): jnp.sum(push * push)  29.4 us
  transfers between devices with their start and end apart: 67, of which 27 were waited for; matrix products, arithmetic and copies ran while one was open for 4% of the time, Pallas kernels for 0%

commit v1 on v0

--- a/solution.py
+++ b/solution.py
@@ -13,6 +13,22 @@
 EPSILON = 1e-06
 SPEED_CAP = 0.1
 PRECISE = lax.Precision.HIGHEST
+
+
+def exchange_in_pairs(value, axis, split, join):
+    ways, here = (lax.axis_size(axis), lax.axis_index(axis))
+    width = value.shape[split] // ways
+    shape = list(value.shape)
+    shape[split] = width
+    height = shape[join]
+    shape[join] = height * ways
+    full = jnp.zeros(shape, value.dtype)
+    for mask in range(ways):
+        part = lax.dynamic_slice_in_dim(value, (here ^ mask) * width, width, axis=split)
+        if mask:
+            part = lax.ppermute(part, axis, [(d, d ^ mask) for d in range(ways)])
+        full = lax.dynamic_update_slice_in_dim(full, part, (here ^ mask) * height, axis=join)
+    return full
 
 
 def with_halo(array, sides, width):
@@ -119,7 +135,7 @@
     shifts_both = jnp.stack([shift_y, shift_x], axis=1)
     send_shift = jnp.dot(placer, shifts_both, precision=PRECISE).reshape(tiles, capacity, 2)
     send_select = jnp.dot(placer, slot_hot, precision=PRECISE).reshape(tiles, capacity, SPAN_DEV)
-    blocks_in = lax.all_to_all(send_blocks, "tile", split_axis=0, concat_axis=0, tiled=True)
+    blocks_in = exchange_in_pairs(send_blocks, "tile", 0, 0)
     shift_in = lax.all_to_all(send_shift, "tile", split_axis=0, concat_axis=0, tiled=True)
     select_in = lax.all_to_all(send_select, "tile", split_axis=0, concat_axis=0, tiled=True)
     sources = blocks_in.shape[0]

time: 1120 us -> 1070 us (0.955)
  waiting for transfers between devices: 109 us -> 9.52 us
  local copies, waits for them, and re-layouts: 26 us -> 43.2 us
  blocking collectives: 676 us -> 691 us
    all_to_all x1 -> x0, waiting for transfers between devices: 93.7 us -> none  [body(): lax.all_to_all(send_blocks, 'tile', split_axis=0, concat_axis=0, tiled=True)]
    psum x16, blocking collectives: 676 us -> 691 us  [body(): lax.psum((jnp.sum(velocity * velocity), jnp.sum(push * push)), ('sec', 't...]
    dynamic_update_slice x0 -> x8, local copies, waits for them, and re-layouts: none -> 14.1 us  [exchange_in_pairs(): lax.dynamic_update_slice_in_dim(full, part, (here ^ mask) * height, axis=...]
  transfers between devices with their start and end apart: 67 -> 73, of which waited for: 27 -> 11; matrix products, arithmetic and copies ran while one was open for 4% -> 10% of each run, Pallas kernels for 0% -> 0%
where the time goes in v1:
time: 1070 us; the launch traced here: 1060 us
  blocking collectives  691 us (65%)
  starting transfers between devices  173 us (16%)
  other arithmetic  55.9 us (5%)
  between operations  45.6 us (4%)
  local copies, waits for them, and re-layouts  43.2 us (4%)
  matrix products  39.7 us (4%)
    psum x16, blocking collectives, body(): lax.psum((jnp.sum(velocity * velocity), jnp.sum(push * push)), ('sec', 't...  691 us
    ppermute x32, starting transfers between devices, with_halo(): before = lax.ppermute(last, axis, up)  117 us
    ppermute x32, starting transfers between devices, with_halo(): after = lax.ppermute(leading, axis, down)  41.3 us
    reduce_sum x16, other arithmetic, body(): jnp.sum(push * push)  32.4 us
  transfers between devices with their start and end apart: 73, of which 11 were waited for; matrix products, arithmetic and copies ran while one was open for 10% of the time, Pallas kernels for 0%

profile of v1, /device:TPU:0, one launch (start us, length us, event | category | flops | bytes accessed | tf_op | source)
XLA Modules:
  0.0 1058.6 jit_solution(11147196865366842248)
XLA Ops:
  1.6 4.9 collective-permute-start.2
  10.1 4.4 fusion.20
  29.0 44.2 %all-reduce.31 = (f32[]{:T(128)}, f32[]{:T(128)}) all-reduce(f32[]{:T(128)} %get-tuple-element.41, f32[]{:T(128)} %get-tuple-element.40), channel_id=1, replica_groups=mesh['sec'=4,'tile'=8] {'sec','tile'}, use_global_device_ids=true, to_apply=%region_1.2 | all-reduce | flops 2 | bytes 16 | tf_op jit(solution)/shard_map/psum | solution.py:104
  96.6 42.2 %all-reduce.30 = (f32[]{:T(128)}, f32[]{:T(128)}) all-reduce(f32[]{:T(128)} %get-tuple-element.39, f32[]{:T(128)} %get-tuple-element.38), channel_id=1, replica_groups=mesh['sec'=4,'tile'=8] {'sec','tile'}, use_global_device_ids=true, to_apply=%region_5.6 | all-reduce | flops 2 | bytes 16 | tf_op jit(solution)/shard_map/psum | solution.py:104
  143.1 4.2 collective-permute-start.10
  158.7 42.1 %all-reduce.29 = (f32[]{:T(128)}, f32[]{:T(128)}) all-reduce(f32[]{:T(128)} %get-tuple-element.37, f32[]{:T(128)} %get-tuple-element.36), channel_id=1, replica_groups=mesh['sec'=4,'tile'=8] {'sec','tile'}, use_global_device_ids=true, to_apply=%region_9.10 | all-reduce | flops 2 | bytes 16 | tf_op jit(solution)/shard_map/psum | solution.py:104
  203.8 4.2 collective-permute-start.14
  216.9 41.6 %all-reduce.28 = (f32[]{:T(128)}, f32[]{:T(128)}) all-reduce(f32[]{:T(128)} %get-tuple-element.35, f32[]{:T(128)} %get-tuple-element.34), channel_id=1, replica_groups=mesh['sec'=4,'tile'=8] {'sec','tile'}, use_global_device_ids=true, to_apply=%region_13.14 | all-reduce | flops 2 | bytes 16 | tf_op jit(solution)/shard_map/psum | solution.py:104
  261.5 4.2 collective-permute-start.18
  274.8 42.6 %all-reduce.27 = (f32[]{:T(128)}, f32[]{:T(128)}) all-reduce(f32[]{:T(128)} %get-tuple-element.33, f32[]{:T(128)} %get-tuple-element.32), channel_id=1, replica_groups=mesh['sec'=4,'tile'=8] {'sec','tile'}, use_global_device_ids=true, to_apply=%region_17.18 | all-reduce | flops 2 | bytes 16 | tf_op jit(solution)/shard_map/psum | solution.py:104
  320.2 4.2 collective-permute-start.22
  333.5 41.4 %all-reduce.26 = (f32[]{:T(128)}, f32[]{:T(128)}) all-reduce(f32[]{:T(128)} %get-tuple-element.31, f32[]{:T(128)} %get-tuple-element.30), channel_id=1, replica_groups=mesh['sec'=4,'tile'=8] {'sec','tile'}, use_global_device_ids=true, to_apply=%region_21.22 | all-reduce | flops 2 | bytes 16 | tf_op jit(solution)/shard_map/psum | solution.py:104
  390.8 42.7 %all-reduce.25 = (f32[]{:T(128)}, f32[]{:T(128)}) all-reduce(f32[]{:T(128)} %get-tuple-element.29, f32[]{:T(128)} %get-tuple-element.28), channel_id=1, replica_groups=mesh['sec'=4,'tile'=8] {'sec','tile'}, use_global_device_ids=true, to_apply=%region_25.26 | all-reduce | flops 2 | bytes 16 | tf_op jit(solution)/shard_map/psum | solution.py:104
  449.5 41.4 %all-reduce.24 = (f32[]{:T(128)}, f32[]{:T(128)}) all-reduce(f32[]{:T(128)} %get-tuple-element.27, f32[]{:T(128)} %get-tuple-element.26), channel_id=1, replica_groups=mesh['sec'=4,'tile'=8] {'sec','tile'}, use_global_device_ids=true, to_apply=%region_29.30 | all-reduce | flops 2 | bytes 16 | tf_op jit(solution)/shard_map/psum | solution.py:104
  506.7 42.8 %all-reduce.23 = (f32[]{:T(128)}, f32[]{:T(128)}) all-reduce(f32[]{:T(128)} %get-tuple-element.25, f32[]{:T(128)} %get-tuple-element.24), channel_id=1, replica_groups=mesh['sec'=4,'tile'=8] {'sec','tile'}, use_global_device_ids=true, to_apply=%region_33.34 | all-reduce | flops 2 | bytes 16 | tf_op jit(solution)/shard_map/psum | solution.py:104
  572.4 42.1 %all-reduce.22 = (f32[]{:T(128)}, f32[]{:T(128)}) all-reduce(f32[]{:T(128)} %get-tuple-element.23, f32[]{:T(128)} %get-tuple-element.22), channel_id=1, replica_groups=mesh['sec'=4,'tile'=8] {'sec','tile'}, use_global_device_ids=true, to_apply=%region_37.38 | all-reduce | flops 2 | bytes 16 | tf_op jit(solution)/shard_map/psum | solution.py:104
  618.0 4.2 collective-permute-start.42
  633.1 51.2 %all-reduce.21 = (f32[]{:T(128)}, f32[]{:T(128)}) all-reduce(f32[]{:T(128)} %get-tuple-element.21, f32[]{:T(128)} %get-tuple-element.20), channel_id=1, replica_groups=mesh['sec'=4,'tile'=8] {'sec','tile'}, use_global_device_ids=true, to_apply=%region_41.42 | all-reduce | flops 2 | bytes 16 | tf_op jit(solution)/shard_map/psum | solution.py:104
  704.0 44.3 %all-reduce.20 = (f32[]{:T(128)}, f32[]{:T(128)}) all-reduce(f32[]{:T(128)} %get-tuple-element.19, f32[]{:T(128)} %get-tuple-element.18), channel_id=1, replica_groups=mesh['sec'=4,'tile'=8] {'sec','tile'}, use_global_device_ids=true, to_apply=%region_45.46 | all-reduce | flops 2 | bytes 16 | tf_op jit(solution)/shard_map/psum | solution.py:104
  751.9 4.2 collective-permute-start.50
  768.2 43.7 %all-reduce.19 = (f32[]{:T(128)}, f32[]{:T(128)}) all-reduce(f32[]{:T(128)} %get-tuple-element.17, f32[]{:T(128)} %get-tuple-element.16), channel_id=1, replica_groups=mesh['sec'=4,'tile'=8] {'sec','tile'}, use_global_device_ids=true, to_apply=%region_49.50 | all-reduce | flops 2 | bytes 16 | tf_op jit(solution)/shard_map/psum | solution.py:104
  815.5 4.2 collective-permute-start.54
  831.1 43.0 %all-reduce.18 = (f32[]{:T(128)}, f32[]{:T(128)}) all-reduce(f32[]{:T(128)} %get-tuple-element.15, f32[]{:T(128)} %get-tuple-element.14), channel_id=1, replica_groups=mesh['sec'=4,'tile'=8] {'sec','tile'}, use_global_device_ids=true, to_apply=%region_53.54 | all-reduce | flops 2 | bytes 16 | tf_op jit(solution)/shard_map/psum | solution.py:104
  877.9 4.2 collective-permute-start.58
  892.6 44.6 %all-reduce.17 = (f32[]{:T(128)}, f32[]{:T(128)}) all-reduce(f32[]{:T(128)} %get-tuple-element.13, f32[]{:T(128)} %get-tuple-element.12), channel_id=1, replica_groups=mesh['sec'=4,'tile'=8] {'sec','tile'}, use_global_device_ids=true, to_apply=%region_57.58 | all-reduce | flops 2 | bytes 16 | tf_op jit(solution)/shard_map/psum | solution.py:104
  940.0 4.2 collective-permute-start.62
  953.4 41.4 %all-reduce.16 = (f32[]{:T(128)}, f32[]{:T(128)}) all-reduce(f32[]{:T(128)} %get-tuple-element.11, f32[]{:T(128)} %get-tuple-element.10), channel_id=1, replica_groups=mesh['sec'=4,'tile'=8] {'sec','tile'}, use_global_device_ids=true, to_apply=%region_61.62 | all-reduce | flops 2 | bytes 16 | tf_op jit(solution)/shard_map/psum | solution.py:104
  997.6 8.6 copy.47
  1006.2 6.4 gather_fusion
  1023.3 10.5 fusion.2
  1033.8 12.1 %fusion.7 = f32[16,384,384]{2,1,0:T(8,128)S(1)} fusion(f32[16,256,384]{2,1,0:T(8,128)S(1)} %fusion.2, f32[16]{0:T(128)S(1)} %sub.587, f32[384,256]{1,0:T(8,128)S(1)} %broadcast_subtract_fusion), kind=kOutput, calls=%fused_computation.8 | convolution fusion | flops 7254048768 | bytes 16121920 | tf_op jit(solution)/shard_map/bri,bik->brk/dot_general | solution.py:76
  1045.9 11.2 %fusion.23 = f32[2,384,384]{2,0,1:T(2,128)S(1)} fusion(f32[8,2,384,384]{3,2,1,0:T(8,128)S(1)} %bitcast.214, f32[8,2,2]{0,2,1:T(2,128)S(1)} %copy-done.6), kind=kOutput, calls=%fused_computation.24 | convolution fusion | flops 56623104 | bytes 10616960 | tf_op jit(solution)/shard_map/skc,skrq->kcrq/dot_general | solution.py:149
  (271 shorter events, 226.1 us)
Async XLA Ops:
  1.6 20.4 %collective-permute-start.2 = (f32[2,2,32,256]{3,2,1,0:T(8,128)S(1)}, f32[2,2,32,256]{3,2,1,0:T(8,128)S(1)}, u32[]{:S(2)}, u32[]{:S(2)}) collective-permute-start(f32[2,2,32,256]{3,2,1,0:T(8,128)S(1)} %get-tuple-element.213), channel_id=1, source_target_pairs={{0,8},{8,16},{16,24},{1,9},{9,17},{17,25},{2,10},{10,18},{18,26},{... | collective-permute-start | bytes 393224 | tf_op jit(solution)/shard_map/ppermute | solution.py:41
  6.5 20.0 %collective-permute-start.3 = (f32[2,2,32,256]{3,2,1,0:T(8,128)S(1)}, f32[2,2,32,256]{3,2,1,0:T(8,128)S(1)}, u32[]{:S(2)}, u32[]{:S(2)}) collective-permute-start(f32[2,2,32,256]{3,2,1,0:T(8,128)S(1)} %get-tuple-element.214), channel_id=1, source_target_pairs={{8,0},{16,8},{24,16},{9,1},{17,9},{25,17},{10,2},{18,10},{26,18},{... | collective-permute-start | bytes 393224 | tf_op jit(solution)/shard_map/ppermute | solution.py:42
  18.5 606.3 %collective-permute-start.64 = (f32[1,2,256,256]{3,0,2,1:T(1,128)}, f32[1,2,256,256]{3,0,2,1:T(1,128)}, u32[]{:S(2)}, u32[]{:S(2)}) collective-permute-start(f32[1,2,256,256]{3,0,2,1:T(1,128)} %get-tuple-element.142), channel_id=1, source_target_pairs={{0,1},{1,0},{2,3},{3,2},{4,5},{5,4},{6,7},{7,6},{8,9},{9,8},{10,11... | collective-permute-start | bytes 1572872 | tf_op jit(solution)/shard_map/ppermute | solution.py:29
  76.5 16.4 %collective-permute-start.6 = (f32[2,2,32,256]{3,2,1,0:T(8,128)}, f32[2,2,32,256]{3,2,1,0:T(8,128)S(1)}, u32[]{:S(2)}, u32[]{:S(2)}) collective-permute-start(f32[2,2,32,256]{3,2,1,0:T(8,128)} %get-tuple-element.208), channel_id=1, source_target_pairs={{0,8},{8,16},{16,24},{1,9},{9,17},{17,25},{2,10},{10,18},{18,26},{... | collective-permute-start | bytes 393224 | tf_op jit(solution)/shard_map/ppermute | solution.py:41
  80.7 12.3 %collective-permute-start.7 = (f32[2,2,32,256]{3,2,1,0:T(8,128)S(1)}, f32[2,2,32,256]{3,2,1,0:T(8,128)S(1)}, u32[]{:S(2)}, u32[]{:S(2)}) collective-permute-start(f32[2,2,32,256]{3,2,1,0:T(8,128)S(1)} %get-tuple-element.209), channel_id=1, source_target_pairs={{8,0},{16,8},{24,16},{9,1},{17,9},{25,17},{10,2},{18,10},{26,18},{... | collective-permute-start | bytes 393224 | tf_op jit(solution)/shard_map/ppermute | solution.py:42
  82.6 10.3 collective-permute-start.4
  89.0 479.8 %all-to-all-start = ((f32[8,2,2]{2,1,0:T(2,128)}), f32[8,2,2]{2,1,0:T(2,128)S(1)}, u32[]{:S(2)}, u32[]{:S(2)}) async-start(f32[8,2,2]{2,1,0:T(2,128)} %bitcast.217), calls=%async_computation | async-start | bytes 16384 | tf_op jit(solution)/shard_map/all_to_all | solution.py:140
  143.1 13.7 %collective-permute-start.10 = (f32[2,2,32,256]{3,2,1,0:T(8,128)S(1)}, f32[2,2,32,256]{3,2,1,0:T(8,128)S(1)}, u32[]{:S(2)}, u32[]{:S(2)}) collective-permute-start(f32[2,2,32,256]{3,2,1,0:T(8,128)S(1)} %get-tuple-element.204), channel_id=1, source_target_pairs={{0,8},{8,16},{16,24},{1,9},{9,17},{17,25},{2,10},{10,18},{18,26},{... | collective-permute-start | bytes 393224 | tf_op jit(solution)/shard_map/ppermute | solution.py:41
  147.3 9.6 collective-permute-start.11
  203.8 10.7 %collective-permute-start.14 = (f32[2,2,32,256]{3,2,1,0:T(8,128)S(1)}, f32[2,2,32,256]{3,2,1,0:T(8,128)S(1)}, u32[]{:S(2)}, u32[]{:S(2)}) collective-permute-start(f32[2,2,32,256]{3,2,1,0:T(8,128)S(1)} %get-tuple-element.200), channel_id=1, source_target_pairs={{0,8},{8,16},{16,24},{1,9},{9,17},{17,25},{2,10},{10,18},{18,26},{... | collective-permute-start | bytes 393224 | tf_op jit(solution)/shard_map/ppermute | solution.py:41
  261.5 10.7 %collective-permute-start.18 = (f32[2,2,32,256]{3,2,1,0:T(8,128)S(1)}, f32[2,2,32,256]{3,2,1,0:T(8,128)S(1)}, u32[]{:S(2)}, u32[]{:S(2)}) collective-permute-start(f32[2,2,32,256]{3,2,1,0:T(8,128)S(1)} %get-tuple-element.196), channel_id=1, source_target_pairs={{0,8},{8,16},{16,24},{1,9},{9,17},{17,25},{2,10},{10,18},{18,26},{... | collective-permute-start | bytes 393224 | tf_op jit(solution)/shard_map/ppermute | solution.py:41
  320.2 10.7 %collective-permute-start.22 = (f32[2,2,32,256]{3,2,1,0:T(8,128)S(1)}, f32[2,2,32,256]{3,2,1,0:T(8,128)S(1)}, u32[]{:S(2)}, u32[]{:S(2)}) collective-permute-start(f32[2,2,32,256]{3,2,1,0:T(8,128)S(1)} %get-tuple-element.192), channel_id=1, source_target_pairs={{0,8},{8,16},{16,24},{1,9},{9,17},{17,25},{2,10},{10,18},{18,26},{... | collective-permute-start | bytes 393224 | tf_op jit(solution)/shard_map/ppermute | solution.py:41
  377.7 11.0 %collective-permute-start.26 = (f32[2,2,32,256]{3,2,1,0:T(8,128)S(1)}, f32[2,2,32,256]{3,2,1,0:T(8,128)S(1)}, u32[]{:S(2)}, u32[]{:S(2)}) collective-permute-start(f32[2,2,32,256]{3,2,1,0:T(8,128)S(1)} %get-tuple-element.188), channel_id=1, source_target_pairs={{0,8},{8,16},{16,24},{1,9},{9,17},{17,25},{2,10},{10,18},{18,26},{... | collective-permute-start | bytes 393224 | tf_op jit(solution)/shard_map/ppermute | solution.py:41
  436.3 11.0 %collective-permute-start.30 = (f32[2,2,32,256]{3,2,1,0:T(8,128)S(1)}, f32[2,2,32,256]{3,2,1,0:T(8,128)S(1)}, u32[]{:S(2)}, u32[]{:S(2)}) collective-permute-start(f32[2,2,32,256]{3,2,1,0:T(8,128)S(1)} %get-tuple-element.184), channel_id=1, source_target_pairs={{0,8},{8,16},{16,24},{1,9},{9,17},{17,25},{2,10},{10,18},{18,26},{... | collective-permute-start | bytes 393224 | tf_op jit(solution)/shard_map/ppermute | solution.py:41
  493.6 11.1 %collective-permute-start.34 = (f32[2,2,32,256]{3,2,1,0:T(8,128)S(1)}, f32[2,2,32,256]{3,2,1,0:T(8,128)S(1)}, u32[]{:S(2)}, u32[]{:S(2)}) collective-permute-start(f32[2,2,32,256]{3,2,1,0:T(8,128)S(1)} %get-tuple-element.180), channel_id=1, source_target_pairs={{0,8},{8,16},{16,24},{1,9},{9,17},{17,25},{2,10},{10,18},{18,26},{... | collective-permute-start | bytes 393224 | tf_op jit(solution)/shard_map/ppermute | solution.py:41
  552.1 17.3 %collective-permute-start.38 = (f32[2,2,32,256]{3,2,1,0:T(8,128)S(1)}, f32[2,2,32,256]{3,2,1,0:T(8,128)S(1)}, u32[]{:S(2)}, u32[]{:S(2)}) collective-permute-start(f32[2,2,32,256]{3,2,1,0:T(8,128)S(1)} %get-tuple-element.176), channel_id=1, source_target_pairs={{0,8},{8,16},{16,24},{1,9},{9,17},{17,25},{2,10},{10,18},{18,26},{... | collective-permute-start | bytes 393224 | tf_op jit(solution)/shard_map/ppermute | solution.py:41
  556.3 13.1 %collective-permute-start.39 = (f32[2,2,32,256]{3,2,1,0:T(8,128)S(1)}, f32[2,2,32,256]{3,2,1,0:T(8,128)S(1)}, u32[]{:S(2)}, u32[]{:S(2)}) collective-permute-start(f32[2,2,32,256]{3,2,1,0:T(8,128)S(1)} %get-tuple-element.177), channel_id=1, source_target_pairs={{8,0},{16,8},{24,16},{9,1},{17,9},{25,17},{10,2},{18,10},{26,18},{... | collective-permute-start | bytes 393224 | tf_op jit(solution)/shard_map/ppermute | solution.py:42
  558.2 11.2 %collective-permute-start.36 = (f32[2,4,1,256]{3,2,1,0:T(1,128)}, f32[2,4,1,256]{3,2,1,0:T(1,128)S(1)}, u32[]{:S(2)}, u32[]{:S(2)}) collective-permute-start(f32[2,4,1,256]{3,2,1,0:T(1,128)} %get-tuple-element.174), channel_id=1, source_target_pairs={{1,0},{2,1},{3,2},{4,3},{5,4},{6,5},{7,6},{9,8},{10,9},{11,10},{12... | collective-permute-start | bytes 24584 | tf_op jit(solution)/shard_map/ppermute | solution.py:42
  559.5 9.9 collective-permute-start.37
  569.4 125.4 %collective-permute-start.65 = (f32[1,2,256,256]{3,0,2,1:T(1,128)}, f32[1,2,256,256]{3,0,2,1:T(1,128)}, u32[]{:S(2)}, u32[]{:S(2)}) collective-permute-start(f32[1,2,256,256]{3,0,2,1:T(1,128)} %get-tuple-element.141), channel_id=1, source_target_pairs={{0,2},{1,3},{2,0},{3,1},{4,6},{5,7},{6,4},{7,5},{8,10},{9,11},{10,... | collective-permute-start | bytes 1572872 | tf_op jit(solution)/shard_map/ppermute | solution.py:29
  618.0 12.7 %collective-permute-start.42 = (f32[2,2,32,256]{3,2,1,0:T(8,128)S(1)}, f32[2,2,32,256]{3,2,1,0:T(8,128)S(1)}, u32[]{:S(2)}, u32[]{:S(2)}) collective-permute-start(f32[2,2,32,256]{3,2,1,0:T(8,128)S(1)} %get-tuple-element.172), channel_id=1, source_target_pairs={{0,8},{8,16},{16,24},{1,9},{9,17},{17,25},{2,10},{10,18},{18,26},{... | collective-permute-start | bytes 393224 | tf_op jit(solution)/shard_map/ppermute | solution.py:41
  629.7 129.0 %collective-permute-start.66 = (f32[1,2,256,256]{3,0,2,1:T(1,128)}, f32[1,2,256,256]{3,0,2,1:T(1,128)}, u32[]{:S(2)}, u32[]{:S(2)}) collective-permute-start(f32[1,2,256,256]{3,0,2,1:T(1,128)} %get-tuple-element.140), channel_id=1, source_target_pairs={{0,3},{1,2},{2,1},{3,0},{4,7},{5,6},{6,5},{7,4},{8,11},{9,10},{10,... | collective-permute-start | bytes 1572872 | tf_op jit(solution)/shard_map/ppermute | solution.py:29
  688.0 13.6 %collective-permute-start.46 = (f32[2,2,32,256]{3,2,1,0:T(8,128)S(1)}, f32[2,2,32,256]{3,2,1,0:T(8,128)S(1)}, u32[]{:S(2)}, u32[]{:S(2)}) collective-permute-start(f32[2,2,32,256]{3,2,1,0:T(8,128)S(1)} %get-tuple-element.168), channel_id=1, source_target_pairs={{0,8},{8,16},{16,24},{1,9},{9,17},{17,25},{2,10},{10,18},{18,26},{... | collective-permute-start | bytes 393224 | tf_op jit(solution)/shard_map/ppermute | solution.py:41
  699.8 122.6 %collective-permute-start.67 = (f32[1,2,256,256]{3,0,2,1:T(1,128)}, f32[1,2,256,256]{3,0,2,1:T(1,128)}, u32[]{:S(2)}, u32[]{:S(2)}) collective-permute-start(f32[1,2,256,256]{3,0,2,1:T(1,128)} %get-tuple-element.139), channel_id=1, source_target_pairs={{0,4},{1,5},{2,6},{3,7},{4,0},{5,1},{6,2},{7,3},{8,12},{9,13},{10,... | collective-permute-start | bytes 1572872 | tf_op jit(solution)/shard_map/ppermute | solution.py:29
  751.9 13.9 %collective-permute-start.50 = (f32[2,2,32,256]{3,2,1,0:T(8,128)S(1)}, f32[2,2,32,256]{3,2,1,0:T(8,128)S(1)}, u32[]{:S(2)}, u32[]{:S(2)}) collective-permute-start(f32[2,2,32,256]{3,2,1,0:T(8,128)S(1)} %get-tuple-element.164), channel_id=1, source_target_pairs={{0,8},{8,16},{16,24},{1,9},{9,17},{17,25},{2,10},{10,18},{18,26},{... | collective-permute-start | bytes 393224 | tf_op jit(solution)/shard_map/ppermute | solution.py:41
  756.1 9.7 collective-permute-start.51
  763.7 121.0 %collective-permute-start.68 = (f32[1,2,256,256]{3,0,2,1:T(1,128)}, f32[1,2,256,256]{3,0,2,1:T(1,128)}, u32[]{:S(2)}, u32[]{:S(2)}) collective-permute-start(f32[1,2,256,256]{3,0,2,1:T(1,128)} %get-tuple-element.138), channel_id=1, source_target_pairs={{0,5},{1,4},{2,7},{3,6},{4,1},{5,0},{6,3},{7,2},{8,13},{9,12},{10,... | collective-permute-start | bytes 1572872 | tf_op jit(solution)/shard_map/ppermute | solution.py:29
  815.5 13.3 %collective-permute-start.54 = (f32[2,2,32,256]{3,2,1,0:T(8,128)S(1)}, f32[2,2,32,256]{3,2,1,0:T(8,128)S(1)}, u32[]{:S(2)}, u32[]{:S(2)}) collective-permute-start(f32[2,2,32,256]{3,2,1,0:T(8,128)S(1)} %get-tuple-element.160), channel_id=1, source_target_pairs={{0,8},{8,16},{16,24},{1,9},{9,17},{17,25},{2,10},{10,18},{18,26},{... | collective-permute-start | bytes 393224 | tf_op jit(solution)/shard_map/ppermute | solution.py:41
  827.3 119.5 %collective-permute-start.69 = (f32[1,2,256,256]{3,0,2,1:T(1,128)}, f32[1,2,256,256]{3,0,2,1:T(1,128)}, u32[]{:S(2)}, u32[]{:S(2)}) collective-permute-start(f32[1,2,256,256]{3,0,2,1:T(1,128)} %get-tuple-element.137), channel_id=1, source_target_pairs={{0,6},{1,7},{2,4},{3,5},{4,2},{5,3},{6,0},{7,1},{8,14},{9,15},{10,... | collective-permute-start | bytes 1572872 | tf_op jit(solution)/shard_map/ppermute | solution.py:29
  877.9 13.1 %collective-permute-start.58 = (f32[2,2,32,256]{3,2,1,0:T(8,128)S(1)}, f32[2,2,32,256]{3,2,1,0:T(8,128)S(1)}, u32[]{:S(2)}, u32[]{:S(2)}) collective-permute-start(f32[2,2,32,256]{3,2,1,0:T(8,128)S(1)} %get-tuple-element.156), channel_id=1, source_target_pairs={{0,8},{8,16},{16,24},{1,9},{9,17},{17,25},{2,10},{10,18},{18,26},{... | collective-permute-start | bytes 393224 | tf_op jit(solution)/shard_map/ppermute | solution.py:41
  889.7 127.8 %collective-permute-start.70 = (f32[1,2,256,256]{3,0,2,1:T(1,128)}, f32[1,2,256,256]{3,0,2,1:T(1,128)}, u32[]{:S(2)}, u32[]{:S(2)}) collective-permute-start(f32[1,2,256,256]{3,0,2,1:T(1,128)} %get-tuple-element.136), channel_id=1, source_target_pairs={{0,7},{1,6},{2,5},{3,4},{4,3},{5,2},{6,1},{7,0},{8,15},{9,14},{10,... | collective-permute-start | bytes 1572872 | tf_op jit(solution)/shard_map/ppermute | solution.py:29
  940.0 11.8 %collective-permute-start.62 = (f32[2,2,32,256]{3,2,1,0:T(8,128)S(1)}, f32[2,2,32,256]{3,2,1,0:T(8,128)S(1)}, u32[]{:S(2)}, u32[]{:S(2)}) collective-permute-start(f32[2,2,32,256]{3,2,1,0:T(8,128)S(1)} %get-tuple-element.152), channel_id=1, source_target_pairs={{0,8},{8,16},{16,24},{1,9},{9,17},{17,25},{2,10},{10,18},{18,26},{... | collective-permute-start | bytes 393224 | tf_op jit(solution)/shard_map/ppermute | solution.py:41
  (55 other events, 735.0 us)
